TPU v7x, 512 devices: a whole 4x8x8 slice. The times are simulated.
512 devices in a mesh: dom: 16 (over x_lo, y), gx: 4 (over x_hi, core), gy: 8 (over z).
Axes of the slice: x: 4 (x_hi: 2, x_lo: 2; x = x_hi * 2 + x_lo), y: 8, z: 8, core: 2. Of those that a mesh axis runs over, the one named last changes fastest.
Arguments:
- ensemble: float32 [16, 4, 32, 32, 1024], P('dom', None, None, 'gx', 'gy'), may hold values from -6 to 6
- ancestors: int32 [16, 4, 128], P(None, 'gx', 'gy'), may hold values from 0 to 15
- particle_air_drag: float32 [16, 2, 32, 1024], P('dom', None, 'gx', 'gy'), may hold values from -6 to 6
- eddy_diffusivity: float32 [31], replicated, may hold values from 0.02 to 0.15
Outputs:
- forecast: float32 [16, 4, 32, 32, 1024], P('dom', None, None, 'gx', 'gy')
All inputs are finite; a program needn't handle non-finite values.
Results may differ from a plain program's by a relative error of at most 0.0003.
Values sent between devices are 32-bit elements; how exact they have to be, the bound alone decides.
No kernel may reach another device: no remote copies, remote signals or barrier semaphores. Data moves between devices by JAX's collectives and lax.ppermute only.
A program may use at most 64 MiB of HBM per device.

v0:
```python
import jax
import jax.numpy as jnp
from jax import lax
from jax.sharding import PartitionSpec as P

STEPS = 4
TILE = 8
ADVECT = 0.2
DIFFUSE = 0.15
BUOY_TEMP = 0.2
BUOY_SALT = 0.1
PRESS_SCALE = 0.25
WIND_SCALE = 0.2
CORIO_BASE = 0.1
CORIO_SLOPE = 0.1


def extended(x, sides, width, wrap):
    for axis, dim in sides:
        size, length = (lax.axis_size(axis), x.shape[dim])
        up = [(i, (i + 1) % size) for i in range(size if wrap else size - 1)]
        down = [(j, i) for i, j in up]
        last = lax.slice_in_dim(x, length - width, length, axis=dim)
        leading = lax.slice_in_dim(x, 0, width, axis=dim)
        before = lax.ppermute(last, axis, up)
        after = lax.ppermute(leading, axis, down)
        x = jnp.concatenate([before, x, after], axis=dim)
    return x


def advance(padded, topmost_slab, eddy_diffusivity, coriolis):
    centre = padded[:, :, 1:-1, 1:-1]
    eastern_neighbour_cell = padded[:, :, 2:, 1:-1]
    west_cell = padded[:, :, :-2, 1:-1]
    north_cell = padded[:, :, 1:-1, 2:]
    south_cell = padded[:, :, 1:-1, :-2]
    grad_x = 0.5 * (eastern_neighbour_cell - west_cell)
    grad_y = 0.5 * (north_cell - south_cell)
    spread = eastern_neighbour_cell + west_cell + north_cell + south_cell - 4.0 * centre
    buoyancy = BUOY_TEMP * padded[2] - BUOY_SALT * padded[3]
    pressure = PRESS_SCALE * jnp.cumsum(buoyancy, axis=0)
    press_x = 0.5 * (pressure[:, 2:, 1:-1] - pressure[:, :-2, 1:-1])
    press_y = 0.5 * (pressure[:, 1:-1, 2:] - pressure[:, 1:-1, :-2])
    vert_flux = eddy_diffusivity[None, :, None, None] * (centre[:, 1:] - centre[:, :-1])
    closed = jnp.zeros_like(centre[:, :1])
    vertical = jnp.concatenate([vert_flux, closed], axis=1) - jnp.concatenate(
        [closed, vert_flux], axis=1
    )
    east_vel = centre[0]
    north_vel = centre[1]
    carried_over = east_vel[None] * grad_x + north_vel[None] * grad_y
    common = centre - ADVECT * carried_over + DIFFUSE * spread + vertical
    level_top = (jnp.arange(centre.shape[1]) == 0).astype(jnp.float32)[:, None, None]
    forcing = WIND_SCALE * topmost_slab[:, None] * level_top
    east_next = common[0] + coriolis * north_vel - press_x + forcing[0]
    north_next = common[1] - coriolis * east_vel - press_y + forcing[1]
    return jnp.stack([east_next, north_next, common[2], common[3]])


def coriolis_at(positions, total_rows):
    return CORIO_BASE + CORIO_SLOPE * (positions.astype(jnp.float32) + 0.5) / total_rows


def per_device(ensemble, ancestors, particle_air_drag, eddy_diffusivity):
    particle_number = lax.axis_index("dom")
    width_y = ensemble.shape[4]
    own_tiles = lax.dynamic_index_in_dim(ancestors, particle_number, 0, keepdims=False)
    cell_source = jnp.repeat(jnp.repeat(own_tiles, TILE, 0), TILE, 1)
    shards = lax.all_gather(ensemble, "dom", axis=0, tiled=True)

    def place(offset, partial_state):
        wanted = (cell_source == offset)[None, None]
        return jnp.where(wanted, shards[offset], partial_state)

    selected_particles = lax.fori_loop(
        0, shards.shape[0], place, jnp.zeros(ensemble.shape[1:], jnp.float32)
    )
    row_block = lax.axis_index("gy")
    total_rows = width_y * lax.axis_size("gy")
    topmost_slab = particle_air_drag[0]
    positions = row_block * width_y + jnp.arange(width_y, dtype=jnp.int32)
    coriolis = coriolis_at(positions, total_rows)
    marine_variables = selected_particles
    for iteration in range(STEPS):
        widened = extended(marine_variables, (("gx", 2),), 1, True)
        padded = extended(widened, (("gy", 3),), 1, False)
        marine_variables = advance(padded, topmost_slab, eddy_diffusivity, coriolis)
    return marine_variables[None]


def solution(mesh):
    placed = (
        P("dom", None, None, "gx", "gy"),
        P(None, "gx", "gy"),
        P("dom", None, "gx", "gy"),
        P(),
    )
    return jax.shard_map(
        per_device,
        mesh=mesh,
        in_specs=placed,
        out_specs=P("dom", None, None, "gx", "gy"),
        check_vma=False,
    )
```

profile of v0, /device:TPU:256, one launch (start us, length us, event | category | flops | bytes accessed | tf_op | source)
XLA Modules:
  0.0 242.3 jit_solution(3216205016897837042)
XLA Ops:
  8.3 106.1 %all-gather.2.cloned.1.call-done = f32[16,4,32,8,128]{4,3,2,1,0:T(8,128)} async-done(((f32[1,4,32,8,128]{4,3,2,1,0:T(8,128)}), f32[16,4,32,8,128]{4,3,2,1,0:T(8,128)}) %all-gather.2.cloned.1.call-update) | async-done | bytes 8388624 | tf_op jit(solution)/shard_map/all_gather | solution.py:69
  114.4 19.9 %while.14 = (s32[]{:T(128)}, f32[4,32,8,128]{3,2,1,0:T(8,128)S(1)}, f32[16,4,32,8,128]{4,3,2,1,0:T(8,128)}, s32[128]{0:T(128)S(1)}, s32[]{:T(128)}, /*index=5*/s32[]{:T(128)}) while((s32[]{:T(128)}, f32[4,32,8,128]{3,2,1,0:T(8,128)S(1)}, f32[16,4,32,8,128]{4,3,2,1,0:T(8,128)}, s32[128]{0:T(128)S(1)}, s32[]{:T(128)}, ...), condition=%wide.region_1.2_spmd.clone, body=%wide.region_0.1_spmd.clone.sunk | while | flops 262275 | bytes 1573719 | solution.py:75
  134.5 3.9 %collective-permute-start = (f32[4,32,1,128]{3,2,1,0:T(1,128)S(1)}, f32[4,32,1,128]{3,2,1,0:T(1,128)S(1)}, u32[]{:S(2)}, u32[]{:S(2)}) collective-permute-start(f32[4,32,1,128]{3,2,1,0:T(1,128)S(1)} %get-tuple-element.148), channel_id=1, source_target_pairs={{8,0},{16,8},{24,16},{0,24},{9,1},{17,9},{25,17},{1,25},{10,2},{18... | collective-permute-start | bytes 196616 | tf_op jit(solution)/shard_map/ppermute | solution.py:26
  138.3 1.9 collective-permute-start.1
  141.2 4.3 %collective-permute-done.1 = f32[4,32,1,128]{3,2,1,0:T(1,128)S(1)} collective-permute-done((f32[4,32,1,128]{3,2,1,0:T(1,128)S(1)}, f32[4,32,1,128]{3,2,1,0:T(1,128)S(1)}, u32[]{:S(2)}, u32[]{:S(2)}) %collective-permute-start.1) | collective-permute-done | bytes 65568 | tf_op jit(solution)/shard_map/ppermute | solution.py:25
  146.4 2.3 collective-permute-start.2
  149.1 3.5 %collective-permute-start.3 = (f32[4,32,10,1]{1,0,3,2:T(4,128)S(1)}, f32[4,32,10,1]{1,0,3,2:T(4,128)S(1)}, u32[]{:S(2)}, u32[]{:S(2)}) collective-permute-start(f32[4,32,10,1]{1,0,3,2:T(4,128)S(1)} %copy.7), channel_id=1, source_target_pairs={{0,1},{1,2},{2,3},{3,4},{4,5},{5,6},{6,7},{8,9},{9,10},{10,11},{11... | collective-permute-start | bytes 15368 | tf_op jit(solution)/shard_map/ppermute | solution.py:25
  153.2 2.7 %collective-permute-done.3 = f32[4,32,10,1]{1,0,3,2:T(4,128)S(1)} collective-permute-done((f32[4,32,10,1]{1,0,3,2:T(4,128)S(1)}, f32[4,32,10,1]{1,0,3,2:T(4,128)S(1)}, u32[]{:S(2)}, u32[]{:S(2)}) %collective-permute-start.3) | collective-permute-done | bytes 5152 | tf_op jit(solution)/shard_map/ppermute | solution.py:25
  156.5 2.2 subtract_add_fusion.3
  160.4 1.9 collective-permute-start.4
  162.4 2.4 collective-permute-start.5
  164.8 4.7 %collective-permute-done.5 = f32[4,32,1,128]{3,2,1,0:T(1,128)S(1)} collective-permute-done((f32[4,32,1,128]{3,2,1,0:T(1,128)S(1)}, f32[4,32,1,128]{3,2,1,0:T(1,128)S(1)}, u32[]{:S(2)}, u32[]{:S(2)}) %collective-permute-start.5) | collective-permute-done | bytes 65568 | tf_op jit(solution)/shard_map/ppermute | solution.py:25
  171.0 1.9 collective-permute-start.6
  173.3 3.9 %collective-permute-start.7 = (f32[4,32,10,1]{1,0,3,2:T(4,128)S(1)}, f32[4,32,10,1]{1,0,3,2:T(4,128)}, u32[]{:S(2)}, u32[]{:S(2)}) collective-permute-start(f32[4,32,10,1]{1,0,3,2:T(4,128)S(1)} %copy.13), channel_id=1, source_target_pairs={{0,1},{1,2},{2,3},{3,4},{4,5},{5,6},{6,7},{8,9},{9,10},{10,11},{11... | collective-permute-start | bytes 15368 | tf_op jit(solution)/shard_map/ppermute | solution.py:25
  178.7 1.6 collective-permute-done.7
  181.5 2.2 subtract_add_fusion.2
  184.9 1.9 collective-permute-start.8
  186.8 2.4 collective-permute-start.9
  189.2 4.7 %collective-permute-done.9 = f32[4,32,1,128]{3,2,1,0:T(1,128)S(1)} collective-permute-done((f32[4,32,1,128]{3,2,1,0:T(1,128)S(1)}, f32[4,32,1,128]{3,2,1,0:T(1,128)S(1)}, u32[]{:S(2)}, u32[]{:S(2)}) %collective-permute-start.9) | collective-permute-done | bytes 65568 | tf_op jit(solution)/shard_map/ppermute | solution.py:25
  194.1 1.3 fusion.130
  195.4 1.6 copy.17
  197.0 1.9 collective-permute-start.10
  199.3 4.1 %collective-permute-start.11 = (f32[4,32,10,1]{1,0,3,2:T(4,128)S(1)}, f32[4,32,10,1]{1,0,3,2:T(4,128)S(1)}, u32[]{:S(2)}, u32[]{:S(2)}) collective-permute-start(f32[4,32,10,1]{1,0,3,2:T(4,128)S(1)} %copy.19), channel_id=1, source_target_pairs={{0,1},{1,2},{2,3},{3,4},{4,5},{5,6},{6,7},{8,9},{9,10},{10,11},{11... | collective-permute-start | bytes 15368 | tf_op jit(solution)/shard_map/ppermute | solution.py:25
  204.8 1.3 collective-permute-done.11
  206.7 2.1 subtract_add_fusion.1
  210.6 1.9 collective-permute-start.12
  212.6 2.4 collective-permute-start.13
  215.0 4.7 %collective-permute-done.13 = f32[4,32,1,128]{3,2,1,0:T(1,128)S(1)} collective-permute-done((f32[4,32,1,128]{3,2,1,0:T(1,128)S(1)}, f32[4,32,1,128]{3,2,1,0:T(1,128)S(1)}, u32[]{:S(2)}, u32[]{:S(2)}) %collective-permute-start.13) | collective-permute-done | bytes 65568 | tf_op jit(solution)/shard_map/ppermute | solution.py:25
  221.2 1.9 collective-permute-start.14
  223.5 3.9 %collective-permute-start.15 = (f32[4,32,10,1]{1,0,3,2:T(4,128)S(1)}, f32[4,32,10,1]{1,0,3,2:T(4,128)}, u32[]{:S(2)}, u32[]{:S(2)}) collective-permute-start(f32[4,32,10,1]{1,0,3,2:T(4,128)S(1)} %copy.25), channel_id=1, source_target_pairs={{0,1},{1,2},{2,3},{3,4},{4,5},{5,6},{6,7},{8,9},{9,10},{10,11},{11... | collective-permute-start | bytes 15368 | tf_op jit(solution)/shard_map/ppermute | solution.py:25
  228.1 2.4 collective-permute-done.15
  231.8 1.8 subtract_add_fusion
  (101 shorter events, 41.9 us)
Async XLA Ops:
  6.5 0.7 copy-start
  6.5 133.7 %copy-start.1 = (f32[31]{0:T(128)S(1)}, f32[31]{0:T(128)}, u32[]{:S(2)}) copy-start(f32[31]{0:T(128)} %param.9) | copy-start | bytes 376
  6.5 107.9 %all-gather.2.cloned.1.call-start = ((), (), s32[]{:S(2)}) async-start(), calls=%async_computation | async-start | bytes 8912896 | tf_op jit(solution)/shard_map/all_gather | solution.py:69
  134.5 6.7 %collective-permute-start = (f32[4,32,1,128]{3,2,1,0:T(1,128)S(1)}, f32[4,32,1,128]{3,2,1,0:T(1,128)S(1)}, u32[]{:S(2)}, u32[]{:S(2)}) collective-permute-start(f32[4,32,1,128]{3,2,1,0:T(1,128)S(1)} %get-tuple-element.148), channel_id=1, source_target_pairs={{8,0},{16,8},{24,16},{0,24},{9,1},{17,9},{25,17},{1,25},{10,2},{18... | collective-permute-start | bytes 196616 | tf_op jit(solution)/shard_map/ppermute | solution.py:26
  138.3 7.1 %collective-permute-start.1 = (f32[4,32,1,128]{3,2,1,0:T(1,128)S(1)}, f32[4,32,1,128]{3,2,1,0:T(1,128)S(1)}, u32[]{:S(2)}, u32[]{:S(2)}) collective-permute-start(f32[4,32,1,128]{3,2,1,0:T(1,128)S(1)} %get-tuple-element.147), channel_id=1, source_target_pairs={{0,8},{8,16},{16,24},{24,0},{1,9},{9,17},{17,25},{25,1},{2,10},{10... | collective-permute-start | bytes 196616 | tf_op jit(solution)/shard_map/ppermute | solution.py:25
  146.4 6.3 %collective-permute-start.2 = (f32[4,32,10,1]{1,0,3,2:T(4,128)S(1)}, f32[4,32,10,1]{1,0,3,2:T(4,128)S(1)}, u32[]{:S(2)}, u32[]{:S(2)}) collective-permute-start(f32[4,32,10,1]{1,0,3,2:T(4,128)S(1)} %copy.5), channel_id=1, source_target_pairs={{1,0},{2,1},{3,2},{4,3},{5,4},{6,5},{7,6},{9,8},{10,9},{11,10},{12... | collective-permute-start | bytes 15368 | tf_op jit(solution)/shard_map/ppermute | solution.py:26
  149.1 6.9 %collective-permute-start.3 = (f32[4,32,10,1]{1,0,3,2:T(4,128)S(1)}, f32[4,32,10,1]{1,0,3,2:T(4,128)S(1)}, u32[]{:S(2)}, u32[]{:S(2)}) collective-permute-start(f32[4,32,10,1]{1,0,3,2:T(4,128)S(1)} %copy.7), channel_id=1, source_target_pairs={{0,1},{1,2},{2,3},{3,4},{4,5},{5,6},{6,7},{8,9},{9,10},{10,11},{11... | collective-permute-start | bytes 15368 | tf_op jit(solution)/shard_map/ppermute | solution.py:25
  160.4 4.3 %collective-permute-start.4 = (f32[4,32,1,128]{3,2,1,0:T(1,128)S(1)}, f32[4,32,1,128]{3,2,1,0:T(1,128)S(1)}, u32[]{:S(2)}, u32[]{:S(2)}) collective-permute-start(f32[4,32,1,128]{3,2,1,0:T(1,128)S(1)} %get-tuple-element.144), channel_id=1, source_target_pairs={{8,0},{16,8},{24,16},{0,24},{9,1},{17,9},{25,17},{1,25},{10,2},{18... | collective-permute-start | bytes 196616 | tf_op jit(solution)/shard_map/ppermute | solution.py:26
  162.4 7.1 %collective-permute-start.5 = (f32[4,32,1,128]{3,2,1,0:T(1,128)S(1)}, f32[4,32,1,128]{3,2,1,0:T(1,128)S(1)}, u32[]{:S(2)}, u32[]{:S(2)}) collective-permute-start(f32[4,32,1,128]{3,2,1,0:T(1,128)S(1)} %get-tuple-element.143), channel_id=1, source_target_pairs={{0,8},{8,16},{16,24},{24,0},{1,9},{9,17},{17,25},{25,1},{2,10},{10... | collective-permute-start | bytes 196616 | tf_op jit(solution)/shard_map/ppermute | solution.py:25
  171.0 7.1 %collective-permute-start.6 = (f32[4,32,10,1]{1,0,3,2:T(4,128)}, f32[4,32,10,1]{1,0,3,2:T(4,128)S(1)}, u32[]{:S(2)}, u32[]{:S(2)}) collective-permute-start(f32[4,32,10,1]{1,0,3,2:T(4,128)} %copy.11), channel_id=1, source_target_pairs={{1,0},{2,1},{3,2},{4,3},{5,4},{6,5},{7,6},{9,8},{10,9},{11,10},{12... | collective-permute-start | bytes 15368 | tf_op jit(solution)/shard_map/ppermute | solution.py:26
  173.3 7.0 %collective-permute-start.7 = (f32[4,32,10,1]{1,0,3,2:T(4,128)S(1)}, f32[4,32,10,1]{1,0,3,2:T(4,128)}, u32[]{:S(2)}, u32[]{:S(2)}) collective-permute-start(f32[4,32,10,1]{1,0,3,2:T(4,128)S(1)} %copy.13), channel_id=1, source_target_pairs={{0,1},{1,2},{2,3},{3,4},{4,5},{5,6},{6,7},{8,9},{9,10},{10,11},{11... | collective-permute-start | bytes 15368 | tf_op jit(solution)/shard_map/ppermute | solution.py:25
  184.9 4.3 %collective-permute-start.8 = (f32[4,32,1,128]{3,2,1,0:T(1,128)S(1)}, f32[4,32,1,128]{3,2,1,0:T(1,128)S(1)}, u32[]{:S(2)}, u32[]{:S(2)}) collective-permute-start(f32[4,32,1,128]{3,2,1,0:T(1,128)S(1)} %get-tuple-element.142), channel_id=1, source_target_pairs={{8,0},{16,8},{24,16},{0,24},{9,1},{17,9},{25,17},{1,25},{10,2},{18... | collective-permute-start | bytes 196616 | tf_op jit(solution)/shard_map/ppermute | solution.py:26
  186.8 7.1 %collective-permute-start.9 = (f32[4,32,1,128]{3,2,1,0:T(1,128)S(1)}, f32[4,32,1,128]{3,2,1,0:T(1,128)S(1)}, u32[]{:S(2)}, u32[]{:S(2)}) collective-permute-start(f32[4,32,1,128]{3,2,1,0:T(1,128)S(1)} %get-tuple-element.141), channel_id=1, source_target_pairs={{0,8},{8,16},{16,24},{24,0},{1,9},{9,17},{17,25},{25,1},{2,10},{10... | collective-permute-start | bytes 196616 | tf_op jit(solution)/shard_map/ppermute | solution.py:25
  197.0 7.3 %collective-permute-start.10 = (f32[4,32,10,1]{1,0,3,2:T(4,128)S(1)}, f32[4,32,10,1]{1,0,3,2:T(4,128)S(1)}, u32[]{:S(2)}, u32[]{:S(2)}) collective-permute-start(f32[4,32,10,1]{1,0,3,2:T(4,128)S(1)} %copy.17), channel_id=1, source_target_pairs={{1,0},{2,1},{3,2},{4,3},{5,4},{6,5},{7,6},{9,8},{10,9},{11,10},{12... | collective-permute-start | bytes 15368 | tf_op jit(solution)/shard_map/ppermute | solution.py:26
  199.3 6.9 %collective-permute-start.11 = (f32[4,32,10,1]{1,0,3,2:T(4,128)S(1)}, f32[4,32,10,1]{1,0,3,2:T(4,128)S(1)}, u32[]{:S(2)}, u32[]{:S(2)}) collective-permute-start(f32[4,32,10,1]{1,0,3,2:T(4,128)S(1)} %copy.19), channel_id=1, source_target_pairs={{0,1},{1,2},{2,3},{3,4},{4,5},{5,6},{6,7},{8,9},{9,10},{10,11},{11... | collective-permute-start | bytes 15368 | tf_op jit(solution)/shard_map/ppermute | solution.py:25
  210.6 4.3 %collective-permute-start.12 = (f32[4,32,1,128]{3,2,1,0:T(1,128)S(1)}, f32[4,32,1,128]{3,2,1,0:T(1,128)S(1)}, u32[]{:S(2)}, u32[]{:S(2)}) collective-permute-start(f32[4,32,1,128]{3,2,1,0:T(1,128)S(1)} %get-tuple-element.140), channel_id=1, source_target_pairs={{8,0},{16,8},{24,16},{0,24},{9,1},{17,9},{25,17},{1,25},{10,2},{18... | collective-permute-start | bytes 196616 | tf_op jit(solution)/shard_map/ppermute | solution.py:26
  212.6 7.1 %collective-permute-start.13 = (f32[4,32,1,128]{3,2,1,0:T(1,128)S(1)}, f32[4,32,1,128]{3,2,1,0:T(1,128)S(1)}, u32[]{:S(2)}, u32[]{:S(2)}) collective-permute-start(f32[4,32,1,128]{3,2,1,0:T(1,128)S(1)} %get-tuple-element.139), channel_id=1, source_target_pairs={{0,8},{8,16},{16,24},{24,0},{1,9},{9,17},{17,25},{25,1},{2,10},{10... | collective-permute-start | bytes 196616 | tf_op jit(solution)/shard_map/ppermute | solution.py:25
  221.2 6.4 %collective-permute-start.14 = (f32[4,32,10,1]{1,0,3,2:T(4,128)}, f32[4,32,10,1]{1,0,3,2:T(4,128)S(1)}, u32[]{:S(2)}, u32[]{:S(2)}) collective-permute-start(f32[4,32,10,1]{1,0,3,2:T(4,128)} %copy.23), channel_id=1, source_target_pairs={{1,0},{2,1},{3,2},{4,3},{5,4},{6,5},{7,6},{9,8},{10,9},{11,10},{12... | collective-permute-start | bytes 15368 | tf_op jit(solution)/shard_map/ppermute | solution.py:26
  223.5 7.0 %collective-permute-start.15 = (f32[4,32,10,1]{1,0,3,2:T(4,128)S(1)}, f32[4,32,10,1]{1,0,3,2:T(4,128)}, u32[]{:S(2)}, u32[]{:S(2)}) collective-permute-start(f32[4,32,10,1]{1,0,3,2:T(4,128)S(1)} %copy.25), channel_id=1, source_target_pairs={{0,1},{1,2},{2,3},{3,4},{4,5},{5,6},{6,7},{8,9},{9,10},{10,11},{11... | collective-permute-start | bytes 15368 | tf_op jit(solution)/shard_map/ppermute | solution.py:25
Sparse Core Ops, SparseCore 0:
  9.4 104.9 all-gather.1
where the time goes:
time: 244 us; the launch traced here: 242 us
  waiting for transfers between devices  133 us (55%)
  starting transfers between devices  42.2 us (17%)
  other arithmetic  38.3 us (16%)
  local copies, waits for them, and re-layouts  14.2 us (6%)
  between operations  13.9 us (6%)
    all_gather x1, waiting for transfers between devices, per_device(): shards = lax.all_gather(ensemble, 'dom', axis=0, tiled=True)  106 us
    ppermute x8, waiting for transfers between devices, extended(): before = lax.ppermute(last, axis, up)  26.4 us
    ppermute x8, starting transfers between devices, extended(): before = lax.ppermute(last, axis, up)  24.6 us
    select_n x16, other arithmetic, place(): return jnp.where(wanted, shards[offset], partial_state)  19.4 us
    ppermute x8, starting transfers between devices, extended(): after = lax.ppermute(leading, axis, down)  17.6 us
    add x4, other arithmetic, advance(): common = centre - ADVECT * carried_over + DIFFUSE * spread + vertical  8.36 us
  transfers between devices with their start and end apart: 17, of which 9 were waited for; matrix products, arithmetic and copies ran while one was open for 3% of the time, Pallas kernels for 0%

commit v1 on v0

--- a/solution.py
+++ b/solution.py
@@ -66,7 +66,9 @@
     width_y = ensemble.shape[4]
     own_tiles = lax.dynamic_index_in_dim(ancestors, particle_number, 0, keepdims=False)
     cell_source = jnp.repeat(jnp.repeat(own_tiles, TILE, 0), TILE, 1)
-    shards = lax.all_gather(ensemble, "dom", axis=0, tiled=True)
+    shards = jnp.concatenate(
+        lax.all_to_all(jnp.stack([ensemble] * lax.axis_size("dom")), "dom", 0, 0), axis=0
+    )
 
     def place(offset, partial_state):
         wanted = (cell_source == offset)[None, None]

time: 244 us -> 324 us (1.33)
  the two profiles are of different devices: /device:TPU:256 before, /device:TPU:296 now
where the time goes in v1:
time: 324 us; the launch traced here: 323 us
  waiting for transfers between devices  215 us (66%)
  starting transfers between devices  49.9 us (15%)
  other arithmetic  37.5 us (12%)
  local copies, waits for them, and re-layouts  19.5 us (6%)
    all_to_all x1, waiting for transfers between devices, per_device(): lax.all_to_all(jnp.stack([ensemble] * lax.axis_size('dom')), 'dom', 0, 0)  189 us
    ppermute x8, waiting for transfers between devices, extended(): before = lax.ppermute(last, axis, up)  26 us
    ppermute x8, starting transfers between devices, extended(): before = lax.ppermute(last, axis, up)  25 us
    select_n x16, other arithmetic, place(): return jnp.where(wanted, shards[offset], partial_state)  19.4 us
    ppermute x8, starting transfers between devices, extended(): after = lax.ppermute(leading, axis, down)  16.8 us
    add x4, other arithmetic, advance(): common = centre - ADVECT * carried_over + DIFFUSE * spread + vertical  8.3 us
    all_to_all x1, starting transfers between devices, per_device(): lax.all_to_all(jnp.stack([ensemble] * lax.axis_size('dom')), 'dom', 0, 0)  8.17 us
  transfers between devices with their start and end apart: 17, of which 9 were waited for; matrix products, arithmetic and copies ran while one was open for 2% of the time, Pallas kernels for 0%

profile of v1, /device:TPU:296, one launch (start us, length us, event | category | flops | bytes accessed | tf_op | source)
XLA Modules:
  0.0 322.5 jit_solution(6651523206507935797)
XLA Ops:
  0.0 5.3 %stack.59 = f32[16,1,4,32,8,128]{5,4,3,2,1,0:T(8,128)} broadcast(f32[4,32,8,128]{3,2,1,0:T(8,128)} %bitcast.150), dimensions={2,3,4,5} | broadcast | bytes 8912896 | tf_op jit(solution)/shard_map/stack | solution.py:70
  5.3 8.2 %all-to-all-start = ((f32[16,1,4,32,8,128]{5,4,3,2,1,0:T(8,128)}), f32[16,1,4,32,8,128]{5,4,3,2,1,0:T(8,128)}, u32[]{:S(2)}, u32[]{:S(2)}) async-start(f32[16,1,4,32,8,128]{5,4,3,2,1,0:T(8,128)} %stack.59), calls=%async_computation | async-start | bytes 16777216 | tf_op jit(solution)/shard_map/all_to_all | solution.py:70
  13.8 188.6 %all-to-all-done = f32[16,1,4,32,8,128]{5,4,3,2,1,0:T(8,128)} async-done(((f32[16,1,4,32,8,128]{5,4,3,2,1,0:T(8,128)}), f32[16,1,4,32,8,128]{5,4,3,2,1,0:T(8,128)}, u32[]{:S(2)}, u32[]{:S(2)}) %all-to-all-start) | async-done | bytes 8388640 | tf_op jit(solution)/shard_map/all_to_all | solution.py:70
  202.5 19.9 %while.14 = (s32[]{:T(128)}, f32[4,32,8,128]{3,2,1,0:T(8,128)S(1)}, f32[16,4,32,8,128]{4,3,2,1,0:T(8,128)}, s32[128]{0:T(128)S(1)}, s32[]{:T(128)}, /*index=5*/s32[]{:T(128)}) while((s32[]{:T(128)}, f32[4,32,8,128]{3,2,1,0:T(8,128)S(1)}, f32[16,4,32,8,128]{4,3,2,1,0:T(8,128)}, s32[128]{0:T(128)S(1)}, s32[]{:T(128)}, ...), condition=%wide.region_1.2_spmd.clone, body=%wide.region_0.1_spmd.clone.sunk | while | flops 262275 | bytes 1573719 | solution.py:77
  222.5 3.4 %collective-permute-start = (f32[4,32,1,128]{3,2,1,0:T(1,128)S(1)}, f32[4,32,1,128]{3,2,1,0:T(1,128)S(1)}, u32[]{:S(2)}, u32[]{:S(2)}) collective-permute-start(f32[4,32,1,128]{3,2,1,0:T(1,128)S(1)} %get-tuple-element.148), channel_id=1, source_target_pairs={{8,0},{16,8},{24,16},{0,24},{9,1},{17,9},{25,17},{1,25},{10,2},{18... | collective-permute-start | bytes 196616 | tf_op jit(solution)/shard_map/ppermute | solution.py:26
  225.9 1.9 collective-permute-start.1
  228.7 4.3 %collective-permute-done.1 = f32[4,32,1,128]{3,2,1,0:T(1,128)S(1)} collective-permute-done((f32[4,32,1,128]{3,2,1,0:T(1,128)S(1)}, f32[4,32,1,128]{3,2,1,0:T(1,128)S(1)}, u32[]{:S(2)}, u32[]{:S(2)}) %collective-permute-start.1) | collective-permute-done | bytes 65568 | tf_op jit(solution)/shard_map/ppermute | solution.py:25
  233.9 1.9 collective-permute-start.2
  236.2 3.9 %collective-permute-start.3 = (f32[4,32,10,1]{1,0,3,2:T(4,128)S(1)}, f32[4,32,10,1]{1,0,3,2:T(4,128)S(1)}, u32[]{:S(2)}, u32[]{:S(2)}) collective-permute-start(f32[4,32,10,1]{1,0,3,2:T(4,128)S(1)} %copy.7), channel_id=1, source_target_pairs={{0,1},{1,2},{2,3},{3,4},{4,5},{5,6},{6,7},{8,9},{9,10},{10,11},{11... | collective-permute-start | bytes 15368 | tf_op jit(solution)/shard_map/ppermute | solution.py:25
  240.7 2.4 collective-permute-done.3
  243.7 2.1 subtract_add_fusion.3
  247.6 1.9 collective-permute-start.4
  249.5 2.4 collective-permute-start.5
  252.0 4.7 %collective-permute-done.5 = f32[4,32,1,128]{3,2,1,0:T(1,128)S(1)} collective-permute-done((f32[4,32,1,128]{3,2,1,0:T(1,128)S(1)}, f32[4,32,1,128]{3,2,1,0:T(1,128)S(1)}, u32[]{:S(2)}, u32[]{:S(2)}) %collective-permute-start.5) | collective-permute-done | bytes 65568 | tf_op jit(solution)/shard_map/ppermute | solution.py:25
  258.1 1.9 collective-permute-start.6
  260.5 3.9 %collective-permute-start.7 = (f32[4,32,10,1]{1,0,3,2:T(4,128)S(1)}, f32[4,32,10,1]{1,0,3,2:T(4,128)}, u32[]{:S(2)}, u32[]{:S(2)}) collective-permute-start(f32[4,32,10,1]{1,0,3,2:T(4,128)S(1)} %copy.13), channel_id=1, source_target_pairs={{0,1},{1,2},{2,3},{3,4},{4,5},{5,6},{6,7},{8,9},{9,10},{10,11},{11... | collective-permute-start | bytes 15368 | tf_op jit(solution)/shard_map/ppermute | solution.py:25
  265.8 1.6 collective-permute-done.7
  268.7 2.2 subtract_add_fusion.2
  272.0 1.9 collective-permute-start.8
  273.9 2.4 collective-permute-start.9
  276.4 4.7 %collective-permute-done.9 = f32[4,32,1,128]{3,2,1,0:T(1,128)S(1)} collective-permute-done((f32[4,32,1,128]{3,2,1,0:T(1,128)S(1)}, f32[4,32,1,128]{3,2,1,0:T(1,128)S(1)}, u32[]{:S(2)}, u32[]{:S(2)}) %collective-permute-start.9) | collective-permute-done | bytes 65568 | tf_op jit(solution)/shard_map/ppermute | solution.py:25
  282.5 1.6 copy.17
  284.1 1.9 collective-permute-start.10
  286.4 4.1 %collective-permute-start.11 = (f32[4,32,10,1]{1,0,3,2:T(4,128)S(1)}, f32[4,32,10,1]{1,0,3,2:T(4,128)S(1)}, u32[]{:S(2)}, u32[]{:S(2)}) collective-permute-start(f32[4,32,10,1]{1,0,3,2:T(4,128)S(1)} %copy.19), channel_id=1, source_target_pairs={{0,1},{1,2},{2,3},{3,4},{4,5},{5,6},{6,7},{8,9},{9,10},{10,11},{11... | collective-permute-start | bytes 15368 | tf_op jit(solution)/shard_map/ppermute | solution.py:25
  293.9 2.1 subtract_add_fusion.1
  297.8 1.9 collective-permute-start.12
  299.7 2.4 collective-permute-start.13
  302.1 4.7 %collective-permute-done.13 = f32[4,32,1,128]{3,2,1,0:T(1,128)S(1)} collective-permute-done((f32[4,32,1,128]{3,2,1,0:T(1,128)S(1)}, f32[4,32,1,128]{3,2,1,0:T(1,128)S(1)}, u32[]{:S(2)}, u32[]{:S(2)}) %collective-permute-start.13) | collective-permute-done | bytes 65568 | tf_op jit(solution)/shard_map/ppermute | solution.py:25
  308.3 1.9 collective-permute-start.14
  310.6 3.9 %collective-permute-start.15 = (f32[4,32,10,1]{1,0,3,2:T(4,128)S(1)}, f32[4,32,10,1]{1,0,3,2:T(4,128)}, u32[]{:S(2)}, u32[]{:S(2)}) collective-permute-start(f32[4,32,10,1]{1,0,3,2:T(4,128)S(1)} %copy.25), channel_id=1, source_target_pairs={{0,1},{1,2},{2,3},{3,4},{4,5},{5,6},{6,7},{8,9},{9,10},{10,11},{11... | collective-permute-start | bytes 15368 | tf_op jit(solution)/shard_map/ppermute | solution.py:25
  315.2 2.4 collective-permute-done.15
  318.9 1.8 subtract_add_fusion
  (103 shorter events, 43.2 us)
Async XLA Ops:
  0.0 13.5 %copy-start = (s32[16,1,16]{2,1,0:T(1,128)S(1)}, s32[16,1,16]{2,1,0:T(1,128)}, u32[]{:S(2)}) copy-start(s32[16,1,16]{2,1,0:T(1,128)} %param.7) | copy-start | bytes 3076
  5.3 8.4 %copy-start.2 = (f32[1,2,8,128]{3,2,1,0:T(8,128)S(1)}, f32[1,2,8,128]{3,2,1,0:T(8,128)}, u32[]{:S(2)}) copy-start(f32[1,2,8,128]{3,2,1,0:T(8,128)} %param.8) | copy-start | bytes 24580
  5.3 197.2 %all-to-all-start = ((f32[16,1,4,32,8,128]{5,4,3,2,1,0:T(8,128)}), f32[16,1,4,32,8,128]{5,4,3,2,1,0:T(8,128)}, u32[]{:S(2)}, u32[]{:S(2)}) async-start(f32[16,1,4,32,8,128]{5,4,3,2,1,0:T(8,128)} %stack.59), calls=%async_computation | async-start | bytes 16777216 | tf_op jit(solution)/shard_map/all_to_all | solution.py:70
  13.5 214.3 %copy-start.1 = (f32[31]{0:T(128)S(1)}, f32[31]{0:T(128)}, u32[]{:S(2)}) copy-start(f32[31]{0:T(128)} %param.9) | copy-start | bytes 376
  222.5 6.2 %collective-permute-start = (f32[4,32,1,128]{3,2,1,0:T(1,128)S(1)}, f32[4,32,1,128]{3,2,1,0:T(1,128)S(1)}, u32[]{:S(2)}, u32[]{:S(2)}) collective-permute-start(f32[4,32,1,128]{3,2,1,0:T(1,128)S(1)} %get-tuple-element.148), channel_id=1, source_target_pairs={{8,0},{16,8},{24,16},{0,24},{9,1},{17,9},{25,17},{1,25},{10,2},{18... | collective-permute-start | bytes 196616 | tf_op jit(solution)/shard_map/ppermute | solution.py:26
  225.9 7.1 %collective-permute-start.1 = (f32[4,32,1,128]{3,2,1,0:T(1,128)S(1)}, f32[4,32,1,128]{3,2,1,0:T(1,128)S(1)}, u32[]{:S(2)}, u32[]{:S(2)}) collective-permute-start(f32[4,32,1,128]{3,2,1,0:T(1,128)S(1)} %get-tuple-element.147), channel_id=1, source_target_pairs={{0,8},{8,16},{16,24},{24,0},{1,9},{9,17},{17,25},{25,1},{2,10},{10... | collective-permute-start | bytes 196616 | tf_op jit(solution)/shard_map/ppermute | solution.py:25
  233.9 6.3 %collective-permute-start.2 = (f32[4,32,10,1]{1,0,3,2:T(4,128)S(1)}, f32[4,32,10,1]{1,0,3,2:T(4,128)S(1)}, u32[]{:S(2)}, u32[]{:S(2)}) collective-permute-start(f32[4,32,10,1]{1,0,3,2:T(4,128)S(1)} %copy.5), channel_id=1, source_target_pairs={{1,0},{2,1},{3,2},{4,3},{5,4},{6,5},{7,6},{9,8},{10,9},{11,10},{12... | collective-permute-start | bytes 15368 | tf_op jit(solution)/shard_map/ppermute | solution.py:26
  236.2 6.9 %collective-permute-start.3 = (f32[4,32,10,1]{1,0,3,2:T(4,128)S(1)}, f32[4,32,10,1]{1,0,3,2:T(4,128)S(1)}, u32[]{:S(2)}, u32[]{:S(2)}) collective-permute-start(f32[4,32,10,1]{1,0,3,2:T(4,128)S(1)} %copy.7), channel_id=1, source_target_pairs={{0,1},{1,2},{2,3},{3,4},{4,5},{5,6},{6,7},{8,9},{9,10},{10,11},{11... | collective-permute-start | bytes 15368 | tf_op jit(solution)/shard_map/ppermute | solution.py:25
  247.6 4.3 %collective-permute-start.4 = (f32[4,32,1,128]{3,2,1,0:T(1,128)S(1)}, f32[4,32,1,128]{3,2,1,0:T(1,128)S(1)}, u32[]{:S(2)}, u32[]{:S(2)}) collective-permute-start(f32[4,32,1,128]{3,2,1,0:T(1,128)S(1)} %get-tuple-element.144), channel_id=1, source_target_pairs={{8,0},{16,8},{24,16},{0,24},{9,1},{17,9},{25,17},{1,25},{10,2},{18... | collective-permute-start | bytes 196616 | tf_op jit(solution)/shard_map/ppermute | solution.py:26
  249.5 7.1 %collective-permute-start.5 = (f32[4,32,1,128]{3,2,1,0:T(1,128)S(1)}, f32[4,32,1,128]{3,2,1,0:T(1,128)S(1)}, u32[]{:S(2)}, u32[]{:S(2)}) collective-permute-start(f32[4,32,1,128]{3,2,1,0:T(1,128)S(1)} %get-tuple-element.143), channel_id=1, source_target_pairs={{0,8},{8,16},{16,24},{24,0},{1,9},{9,17},{17,25},{25,1},{2,10},{10... | collective-permute-start | bytes 196616 | tf_op jit(solution)/shard_map/ppermute | solution.py:25
  258.1 7.1 %collective-permute-start.6 = (f32[4,32,10,1]{1,0,3,2:T(4,128)}, f32[4,32,10,1]{1,0,3,2:T(4,128)S(1)}, u32[]{:S(2)}, u32[]{:S(2)}) collective-permute-start(f32[4,32,10,1]{1,0,3,2:T(4,128)} %copy.11), channel_id=1, source_target_pairs={{1,0},{2,1},{3,2},{4,3},{5,4},{6,5},{7,6},{9,8},{10,9},{11,10},{12... | collective-permute-start | bytes 15368 | tf_op jit(solution)/shard_map/ppermute | solution.py:26
  260.5 7.0 %collective-permute-start.7 = (f32[4,32,10,1]{1,0,3,2:T(4,128)S(1)}, f32[4,32,10,1]{1,0,3,2:T(4,128)}, u32[]{:S(2)}, u32[]{:S(2)}) collective-permute-start(f32[4,32,10,1]{1,0,3,2:T(4,128)S(1)} %copy.13), channel_id=1, source_target_pairs={{0,1},{1,2},{2,3},{3,4},{4,5},{5,6},{6,7},{8,9},{9,10},{10,11},{11... | collective-permute-start | bytes 15368 | tf_op jit(solution)/shard_map/ppermute | solution.py:25
  272.0 4.3 %collective-permute-start.8 = (f32[4,32,1,128]{3,2,1,0:T(1,128)S(1)}, f32[4,32,1,128]{3,2,1,0:T(1,128)S(1)}, u32[]{:S(2)}, u32[]{:S(2)}) collective-permute-start(f32[4,32,1,128]{3,2,1,0:T(1,128)S(1)} %get-tuple-element.142), channel_id=1, source_target_pairs={{8,0},{16,8},{24,16},{0,24},{9,1},{17,9},{25,17},{1,25},{10,2},{18... | collective-permute-start | bytes 196616 | tf_op jit(solution)/shard_map/ppermute | solution.py:26
  273.9 7.1 %collective-permute-start.9 = (f32[4,32,1,128]{3,2,1,0:T(1,128)S(1)}, f32[4,32,1,128]{3,2,1,0:T(1,128)S(1)}, u32[]{:S(2)}, u32[]{:S(2)}) collective-permute-start(f32[4,32,1,128]{3,2,1,0:T(1,128)S(1)} %get-tuple-element.141), channel_id=1, source_target_pairs={{0,8},{8,16},{16,24},{24,0},{1,9},{9,17},{17,25},{25,1},{2,10},{10... | collective-permute-start | bytes 196616 | tf_op jit(solution)/shard_map/ppermute | solution.py:25
  284.1 7.3 %collective-permute-start.10 = (f32[4,32,10,1]{1,0,3,2:T(4,128)S(1)}, f32[4,32,10,1]{1,0,3,2:T(4,128)S(1)}, u32[]{:S(2)}, u32[]{:S(2)}) collective-permute-start(f32[4,32,10,1]{1,0,3,2:T(4,128)S(1)} %copy.17), channel_id=1, source_target_pairs={{1,0},{2,1},{3,2},{4,3},{5,4},{6,5},{7,6},{9,8},{10,9},{11,10},{12... | collective-permute-start | bytes 15368 | tf_op jit(solution)/shard_map/ppermute | solution.py:26
  286.4 6.9 %collective-permute-start.11 = (f32[4,32,10,1]{1,0,3,2:T(4,128)S(1)}, f32[4,32,10,1]{1,0,3,2:T(4,128)S(1)}, u32[]{:S(2)}, u32[]{:S(2)}) collective-permute-start(f32[4,32,10,1]{1,0,3,2:T(4,128)S(1)} %copy.19), channel_id=1, source_target_pairs={{0,1},{1,2},{2,3},{3,4},{4,5},{5,6},{6,7},{8,9},{9,10},{10,11},{11... | collective-permute-start | bytes 15368 | tf_op jit(solution)/shard_map/ppermute | solution.py:25
  297.8 4.3 %collective-permute-start.12 = (f32[4,32,1,128]{3,2,1,0:T(1,128)S(1)}, f32[4,32,1,128]{3,2,1,0:T(1,128)S(1)}, u32[]{:S(2)}, u32[]{:S(2)}) collective-permute-start(f32[4,32,1,128]{3,2,1,0:T(1,128)S(1)} %get-tuple-element.140), channel_id=1, source_target_pairs={{8,0},{16,8},{24,16},{0,24},{9,1},{17,9},{25,17},{1,25},{10,2},{18... | collective-permute-start | bytes 196616 | tf_op jit(solution)/shard_map/ppermute | solution.py:26
  299.7 7.1 %collective-permute-start.13 = (f32[4,32,1,128]{3,2,1,0:T(1,128)S(1)}, f32[4,32,1,128]{3,2,1,0:T(1,128)S(1)}, u32[]{:S(2)}, u32[]{:S(2)}) collective-permute-start(f32[4,32,1,128]{3,2,1,0:T(1,128)S(1)} %get-tuple-element.139), channel_id=1, source_target_pairs={{0,8},{8,16},{16,24},{24,0},{1,9},{9,17},{17,25},{25,1},{2,10},{10... | collective-permute-start | bytes 196616 | tf_op jit(solution)/shard_map/ppermute | solution.py:25
  308.3 6.4 %collective-permute-start.14 = (f32[4,32,10,1]{1,0,3,2:T(4,128)}, f32[4,32,10,1]{1,0,3,2:T(4,128)S(1)}, u32[]{:S(2)}, u32[]{:S(2)}) collective-permute-start(f32[4,32,10,1]{1,0,3,2:T(4,128)} %copy.23), channel_id=1, source_target_pairs={{1,0},{2,1},{3,2},{4,3},{5,4},{6,5},{7,6},{9,8},{10,9},{11,10},{12... | collective-permute-start | bytes 15368 | tf_op jit(solution)/shard_map/ppermute | solution.py:26
  310.6 7.0 %collective-permute-start.15 = (f32[4,32,10,1]{1,0,3,2:T(4,128)S(1)}, f32[4,32,10,1]{1,0,3,2:T(4,128)}, u32[]{:S(2)}, u32[]{:S(2)}) collective-permute-start(f32[4,32,10,1]{1,0,3,2:T(4,128)S(1)} %copy.25), channel_id=1, source_target_pairs={{0,1},{1,2},{2,3},{3,4},{4,5},{5,6},{6,7},{8,9},{9,10},{10,11},{11... | collective-permute-start | bytes 15368 | tf_op jit(solution)/shard_map/ppermute | solution.py:25
